TPU v7x, 32 devices: a whole 2x2x4 slice. The times are simulated.
32 devices in a mesh: row: 4 (over x, core), col: 8 (over z, y).
Axes of the slice: x: 2, y: 2, z: 4, core: 2. Of those that a mesh axis runs over, the one named last changes fastest.
Arguments:
- kernel: bfloat16 [32768, 32768], P('row', 'col'), may hold values from -1 to 1
- random_cols: bfloat16 [32768, 256], P('row'), may hold values from -6 to 6
- tree_perm: int32 [32768], replicated, may hold values from 0 to 32767, as said below
- leaf_units: int32 [32], replicated, may hold values from 1 to 8, 160 in all
Outputs:
- bases: bfloat16 [4, 32768, 256], P(None, ('row', 'col'))
Inputs may be any that keep to these rules, and one draw needn't show every extreme that they name: `tree_perm`: A permutation. Cut tree positions and stored rows alike into blocks of 1024 in order: every tree block takes at most 32 rows from any one stored block, some pair of blocks shares exactly 32, and every stored block gives 1024 rows in all. `leaf_units`: they sum to 160.
All inputs are finite; a program needn't handle non-finite values.
Results may differ from a plain program's by a relative error of at most 0.0067.
Values may be sent and summed in bfloat16 or wider, within the bound.
A program may use at most 192 MiB of HBM per device.

v0:
```python
import jax
import jax.numpy as jnp
from jax import lax
from jax.sharding import PartitionSpec as P

UNIT = 128
MINU = 4
LEVELS = 3


def shards(kernel, random_cols, tree_perm, leaf_units):
    width = random_cols.shape[1]
    partial_w = lax.dot_general(
        kernel, random_cols, (((0,), (0,)), ((), ())), preferred_element_type=jnp.float32
    )
    sample_w = lax.psum(partial_w, "row").astype(jnp.bfloat16)
    columns_count = lax.axis_size("col")
    rows_dev = kernel.shape[0] // columns_count
    sample = lax.psum_scatter(
        jnp.dot(kernel, sample_w, preferred_element_type=jnp.float32),
        "col",
        scatter_dimension=0,
        tiled=True,
    ).astype(jnp.bfloat16)
    devices = lax.axis_size("row") * columns_count
    total_rows = tree_perm.shape[0]
    device = lax.axis_index(("row", "col"))
    offset = device * rows_dev
    wanted = lax.dynamic_slice_in_dim(tree_perm, offset, rows_dev)
    inverse = (
        jnp.zeros((total_rows,), jnp.int32)
        .at[tree_perm]
        .set(jnp.arange(total_rows, dtype=jnp.int32))
    )
    placed = lax.dynamic_slice_in_dim(inverse, offset, rows_dev)
    capacity = (rows_dev + devices - 1) // devices
    target = placed // rows_dev
    ahead_mine = (target[None, :] == target[:, None]) & (placed[None, :] < placed[:, None])
    slot = target * capacity + jnp.sum(ahead_mine, axis=1)
    outgoing = jnp.zeros((devices * capacity, width), jnp.bfloat16).at[slot].set(sample)
    incoming = lax.all_to_all(outgoing, ("row", "col"), split_axis=0, concat_axis=0, tiled=True)
    source = wanted // rows_dev
    order = jnp.arange(rows_dev, dtype=jnp.int32)
    ahead_theirs = (source[None, :] == source[:, None]) & (order[None, :] < order[:, None])
    pick = source * capacity + jnp.sum(ahead_theirs, axis=1)
    tree_rows = jnp.take(incoming, pick, axis=0)
    sizes = UNIT * (MINU - 1 + leaf_units)
    leaves = sizes.shape[0]
    ends = jnp.cumsum(sizes)
    positions = offset + jnp.arange(rows_dev, dtype=jnp.int32)
    leaf_of = jnp.sum(positions[:, None] >= ends[None, :], axis=1)
    reach = rows_dev // (UNIT * MINU) + 2
    offsets = jnp.arange(reach, dtype=jnp.int32)
    levels = LEVELS + 1
    node_ids = [leaf_of // 2**level for level in range(levels)]
    totals = []
    stored_leaf = jnp.sum(placed[:, None] >= ends[None, :], axis=1)
    leaf_range = jnp.arange(leaves, dtype=jnp.int32)
    chosen = stored_leaf[None, :] == leaf_range[:, None]
    masked = jnp.where(chosen[:, :, None], sample[None, :, :], jnp.zeros((), jnp.bfloat16))
    spread = jnp.einsum("lrs,rt->lst", masked, sample, preferred_element_type=jnp.float32)
    leaf_grams = lax.psum(spread, ("row", "col"))
    for level in range(levels):
        group = 2**level
        count = leaves // group
        node_grams = leaf_grams.reshape(count, group, width, width).sum(axis=1)
        index = jnp.minimum(node_ids[level][0] + offsets, count - 1)
        totals.append(jnp.take(node_grams, index, axis=0))
    identity_matrix = jnp.eye(width, dtype=jnp.float32)
    values = tree_rows.astype(jnp.float32).T
    results = []
    for level in range(levels):
        ids = node_ids[level]
        group = 2**level
        count = leaves // group
        node_sizes = sizes.reshape(count, group).sum(axis=1)
        candidate = ids[0] + offsets
        present = candidate <= ids[-1]
        counts = jnp.take(node_sizes, jnp.minimum(candidate, count - 1)).astype(jnp.float32)
        mean = jnp.where(
            present[:, None, None], totals[level] / counts[:, None, None], identity_matrix[None]
        )
        factor = jnp.linalg.cholesky(mean)
        basis = jnp.zeros((rows_dev, width), jnp.float32)
        for which in range(reach):
            solved = jax.scipy.linalg.solve_triangular(factor[which], values, lower=True).T
            basis = basis + jnp.where((ids == candidate[which])[:, None], solved, 0.0)
        results.append(basis.astype(jnp.bfloat16))
    return jnp.stack(results)


def solution(mesh):
    return jax.shard_map(
        shards,
        mesh=mesh,
        in_specs=(P("row", "col"), P("row", None), P(), P()),
        out_specs=P(None, ("row", "col"), None),
        check_vma=False,
    )
```

profile of v0, /device:TPU:0, one launch (start us, length us, event | category | flops | bytes accessed | tf_op | source)
XLA Modules:
  0.0 1622.3 jit_solution(10285654006331508957)
XLA Ops:
  6.5 30.1 %fusion.169 = f32[4096,256]{1,0:T(8,128)} fusion(bf16[8192,4096]{1,0:T(8,128)(2,1)} %param.7, bf16[8192,256]{1,0:T(8,128)(2,1)} %param.8), kind=kOutput, calls=%fused_computation.425 | convolution fusion | flops 17179869184 | bytes 75497472 | tf_op jit(solution)/shard_map/dot_general | solution.py:13
  36.6 78.7 %all-reduce.5 = bf16[4096,256]{1,0:T(8,128)(2,1)S(1)} all-reduce(f32[4096,256]{1,0:T(8,128)} %fusion.169), channel_id=1, replica_groups=mesh['row'=4,'col'=8] {'row'}, use_global_device_ids=true, to_apply=%region_4.5 | all-reduce | flops 1048576 | bytes 6291456 | tf_op jit(solution)/shard_map/psum | solution.py:16
  115.4 30.2 %convolution_bitcast_fusion = f32[8192,256]{0,1:T(8,128)} fusion(bf16[8192,4096]{1,0:T(8,128)(2,1)} %param.7, bf16[4096,256]{1,0:T(8,128)(2,1)S(1)} %all-reduce.5), kind=kOutput, calls=%fused_computation.46 | convolution fusion | flops 17179869184 | bytes 77594624 | tf_op jit(solution)/shard_map/dot_general | solution.py:20
  146.5 120.1 %scatter_custom_fusion = s32[32768]{0:T(1024)S(1)} fusion(s32[32768]{0:T(1024)S(1)} %compare_select_fusion, s32[32768]{0:T(1024)S(1)} %iota.124, s32[]{:T(128)} %copy.190), kind=kCustom, calls=%fused_computation.279 | custom fusion | bytes 131076 | tf_op jit(solution)/shard_map/scatter | solution.py:33
  274.3 19.7 %reduce-scatter.2.cloned.1.call-done = f32[1024,256]{0,1:T(8,128)} async-done(((f32[8192,256]{0,1:T(8,128)}), f32[1024,256]{0,1:T(8,128)}) %reduce-scatter.2.cloned.1.call-update) | async-done | bytes 1048592 | tf_op jit(solution)/shard_map/reduce_scatter | solution.py:19
  295.3 6.8 fusion
  311.6 3.1 broadcast_compare_fusion.18
  323.4 5.7 scatter_custom_fusion.1
  329.1 3.9 all-to-all-start
  333.0 3.1 broadcast_compare_fusion.11
  338.7 5.6 broadcast_compare_fusion.3
  344.3 10.5 all-to-all-done
  354.8 3.9 gather_fusion.2
  359.0 131.6 %all-reduce.4.cloned.1.call-done = f32[32,256,256]{2,1,0:T(8,128)} async-done(((f32[32,256,256]{2,1,0:T(8,128)}), f32[32,256,256]{2,1,0:T(8,128)}) %all-reduce.4.cloned.1.call-update) | async-done | bytes 8388624 | tf_op jit(solution)/shard_map/psum | solution.py:62
  490.7 4.2 bitcast_reduce_fusion.1
  499.0 6.6 bitcast_reduce_fusion.2
  509.7 4.1 bitcast_reduce_fusion
  515.7 4.0 gather_fusion
  521.1 4.1 divide_select_fusion.1
  531.1 47.7 %custom-call.37 = f32[4,128,128]{2,1,0:T(8,128)S(1)} custom-call(f32[4,128,128]{2,1,0:T(8,128)} %cholesky.350), custom_call_target="Cholesky" | custom-call | tf_op jit(solution)/shard_map/jit(cholesky)/cholesky | solution.py:83
  584.8 48.5 %custom-call.51 = f32[4,128,128]{2,1,0:T(8,128)} custom-call(f32[4,128,128]{2,1,0:T(8,128)} %cholesky.356), custom_call_target="Cholesky" | custom-call | tf_op jit(solution)/shard_map/jit(cholesky)/cholesky | solution.py:83
  637.0 47.5 %custom-call.44 = f32[4,128,128]{2,1,0:T(8,128)} custom-call(f32[4,128,128]{2,1,0:T(8,128)S(1)} %cholesky.353), custom_call_target="Cholesky" | custom-call | tf_op jit(solution)/shard_map/jit(cholesky)/cholesky | solution.py:83
  686.0 47.3 %custom-call.58 = f32[4,128,128]{2,1,0:T(8,128)S(1)} custom-call(f32[4,128,128]{2,1,0:T(8,128)S(1)} %cholesky.359), custom_call_target="Cholesky" | custom-call | tf_op jit(solution)/shard_map/jit(cholesky)/cholesky | solution.py:83
  735.4 39.3 %custom-call.38 = f32[4,1,128,128]{2,3,1,0:T(8,128)S(1)} custom-call(f32[4,1,128,128]{3,2,1,0:T(8,128)S(1)} %get-tuple-element.324), custom_call_target="InvertDiagBlocksLowerTriangular" | custom-call | tf_op jit(solution)/shard_map/jit(cholesky)/cholesky | solution.py:83
  777.7 47.5 %custom-call.39 = f32[4,128,128]{2,1,0:T(8,128)} custom-call(f32[4,128,128]{2,1,0:T(8,128)S(1)} %convolution_subtract_fusion.19), custom_call_target="Cholesky" | custom-call | tf_op jit(solution)/shard_map/jit(cholesky)/cholesky | solution.py:83
  826.3 40.9 %custom-call.45 = f32[4,1,128,128]{2,3,1,0:T(8,128)} custom-call(f32[4,1,128,128]{3,2,1,0:T(8,128)} %get-tuple-element.322), custom_call_target="InvertDiagBlocksLowerTriangular" | custom-call | tf_op jit(solution)/shard_map/jit(cholesky)/cholesky | solution.py:83
  871.2 48.3 %custom-call.46 = f32[4,128,128]{2,1,0:T(8,128)} custom-call(f32[4,128,128]{2,1,0:T(8,128)} %convolution_subtract_fusion.18), custom_call_target="Cholesky" | custom-call | tf_op jit(solution)/shard_map/jit(cholesky)/cholesky | solution.py:83
  921.6 40.7 %custom-call.52 = f32[4,1,128,128]{2,3,1,0:T(8,128)} custom-call(f32[4,1,128,128]{3,2,1,0:T(8,128)} %get-tuple-element.321), custom_call_target="InvertDiagBlocksLowerTriangular" | custom-call | tf_op jit(solution)/shard_map/jit(cholesky)/cholesky | solution.py:83
  966.8 48.5 %custom-call.53 = f32[4,128,128]{2,1,0:T(8,128)} custom-call(f32[4,128,128]{2,1,0:T(8,128)} %convolution_subtract_fusion.17), custom_call_target="Cholesky" | custom-call | tf_op jit(solution)/shard_map/jit(cholesky)/cholesky | solution.py:83
  1016.4 40.8 %custom-call.59 = f32[4,1,128,128]{2,3,1,0:T(8,128)} custom-call(f32[4,1,128,128]{3,2,1,0:T(8,128)} %get-tuple-element.323), custom_call_target="InvertDiagBlocksLowerTriangular" | custom-call | tf_op jit(solution)/shard_map/jit(cholesky)/cholesky | solution.py:83
  1060.9 48.3 %custom-call.60 = f32[4,128,128]{2,1,0:T(8,128)} custom-call(f32[4,128,128]{2,1,0:T(8,128)} %convolution_subtract_fusion.16), custom_call_target="Cholesky" | custom-call | tf_op jit(solution)/shard_map/jit(cholesky)/cholesky | solution.py:83
  1112.7 3.5 select_select_fusion.3
  1116.3 3.8 while.47
  1120.1 20.1 %custom-call.64 = f32[2,128,128]{1,2,0:T(8,128)S(1)} custom-call(f32[2,128,128]{2,1,0:T(8,128)S(1)} %get-tuple-element.120), custom_call_target="InvertDiagBlocksLowerTriangular" | custom-call | tf_op jit(solution)/shard_map/jit(_solve_triangular)/triangular_solve | solution.py:86
  1142.9 4.3 while.46
  1147.2 19.7 %custom-call.63 = f32[2,128,128]{1,2,0:T(8,128)S(1)} custom-call(f32[2,128,128]{2,1,0:T(8,128)S(1)} %get-tuple-element.119), custom_call_target="InvertDiagBlocksLowerTriangular" | custom-call | tf_op jit(solution)/shard_map/jit(_solve_triangular)/triangular_solve | solution.py:86
  1169.6 4.0 while.45
  1173.5 19.7 %custom-call.62 = f32[2,128,128]{1,2,0:T(8,128)S(1)} custom-call(f32[2,128,128]{2,1,0:T(8,128)S(1)} %get-tuple-element.118), custom_call_target="InvertDiagBlocksLowerTriangular" | custom-call | tf_op jit(solution)/shard_map/jit(_solve_triangular)/triangular_solve | solution.py:86
  1195.9 4.2 while.44
  1200.7 19.8 %custom-call.61 = f32[2,128,128]{1,2,0:T(8,128)S(1)} custom-call(f32[2,128,128]{2,1,0:T(8,128)S(1)} %get-tuple-element.117), custom_call_target="InvertDiagBlocksLowerTriangular" | custom-call | tf_op jit(solution)/shard_map/jit(_solve_triangular)/triangular_solve | solution.py:86
  1224.1 6.9 while.43
  1231.7 20.5 %custom-call.57 = f32[2,128,128]{1,2,0:T(8,128)S(1)} custom-call(f32[2,128,128]{2,1,0:T(8,128)} %copy-done.47), custom_call_target="InvertDiagBlocksLowerTriangular" | custom-call | tf_op jit(solution)/shard_map/jit(_solve_triangular)/triangular_solve | solution.py:86
  1256.5 7.2 while.42
  1264.4 20.5 %custom-call.56 = f32[2,128,128]{1,2,0:T(8,128)S(1)} custom-call(f32[2,128,128]{2,1,0:T(8,128)} %copy-done.48), custom_call_target="InvertDiagBlocksLowerTriangular" | custom-call | tf_op jit(solution)/shard_map/jit(_solve_triangular)/triangular_solve | solution.py:86
  1289.2 7.1 while.41
  1297.0 20.7 %custom-call.55 = f32[2,128,128]{1,2,0:T(8,128)S(1)} custom-call(f32[2,128,128]{2,1,0:T(8,128)} %copy-done.49), custom_call_target="InvertDiagBlocksLowerTriangular" | custom-call | tf_op jit(solution)/shard_map/jit(_solve_triangular)/triangular_solve | solution.py:86
  1322.0 5.4 while.40
  1328.0 20.5 %custom-call.54 = f32[2,128,128]{1,2,0:T(8,128)S(1)} custom-call(f32[2,128,128]{2,1,0:T(8,128)} %copy-done.50), custom_call_target="InvertDiagBlocksLowerTriangular" | custom-call | tf_op jit(solution)/shard_map/jit(_solve_triangular)/triangular_solve | solution.py:86
  1352.9 6.8 while.39
  1360.4 20.5 %custom-call.50 = f32[2,128,128]{1,2,0:T(8,128)S(1)} custom-call(f32[2,128,128]{2,1,0:T(8,128)} %copy-done.51), custom_call_target="InvertDiagBlocksLowerTriangular" | custom-call | tf_op jit(solution)/shard_map/jit(_solve_triangular)/triangular_solve | solution.py:86
  1385.2 6.8 while.38
  1392.7 20.9 %custom-call.49 = f32[2,128,128]{1,2,0:T(8,128)S(1)} custom-call(f32[2,128,128]{2,1,0:T(8,128)} %copy-done.52), custom_call_target="InvertDiagBlocksLowerTriangular" | custom-call | tf_op jit(solution)/shard_map/jit(_solve_triangular)/triangular_solve | solution.py:86
  1418.0 7.1 while.37
  1425.8 20.5 %custom-call.48 = f32[2,128,128]{1,2,0:T(8,128)S(1)} custom-call(f32[2,128,128]{2,1,0:T(8,128)} %copy-done.53), custom_call_target="InvertDiagBlocksLowerTriangular" | custom-call | tf_op jit(solution)/shard_map/jit(_solve_triangular)/triangular_solve | solution.py:86
  1450.6 5.4 while.36
  1456.6 20.5 %custom-call.47 = f32[2,128,128]{1,2,0:T(8,128)S(1)} custom-call(f32[2,128,128]{2,1,0:T(8,128)} %copy-done.54), custom_call_target="InvertDiagBlocksLowerTriangular" | custom-call | tf_op jit(solution)/shard_map/jit(_solve_triangular)/triangular_solve | solution.py:86
  1481.6 7.1 while.35
  1489.4 20.6 %custom-call.43 = f32[2,128,128]{1,2,0:T(8,128)S(1)} custom-call(f32[2,128,128]{2,1,0:T(8,128)} %copy-done.55), custom_call_target="InvertDiagBlocksLowerTriangular" | custom-call | tf_op jit(solution)/shard_map/jit(_solve_triangular)/triangular_solve | solution.py:86
  1514.3 7.2 while.34
  1522.1 20.5 %custom-call.42 = f32[2,128,128]{1,2,0:T(8,128)S(1)} custom-call(f32[2,128,128]{2,1,0:T(8,128)} %copy-done.56), custom_call_target="InvertDiagBlocksLowerTriangular" | custom-call | tf_op jit(solution)/shard_map/jit(_solve_triangular)/triangular_solve | solution.py:86
  1546.9 6.8 while.33
  1554.4 20.5 %custom-call.41 = f32[2,128,128]{1,2,0:T(8,128)S(1)} custom-call(f32[2,128,128]{2,1,0:T(8,128)} %copy-done.57), custom_call_target="InvertDiagBlocksLowerTriangular" | custom-call | tf_op jit(solution)/shard_map/jit(_solve_triangular)/triangular_solve | solution.py:86
  1579.2 5.4 while.32
  1585.2 20.7 %custom-call.40 = f32[2,128,128]{1,2,0:T(8,128)S(1)} custom-call(f32[2,128,128]{2,1,0:T(8,128)} %copy-done.46), custom_call_target="InvertDiagBlocksLowerTriangular" | custom-call | tf_op jit(solution)/shard_map/jit(_solve_triangular)/triangular_solve | solution.py:86
  (426 shorter events, 255.0 us)
Async XLA Ops:
  6.5 287.5 %reduce-scatter.2.cloned.1.call-start = ((), (), s32[]{:S(2)}) async-start(), calls=%async_computation.2 | async-start | bytes 9437184 | tf_op jit(solution)/shard_map/reduce_scatter | solution.py:19
  145.6 0.9 copy-start.45
  145.6 345.1 %all-reduce.4.cloned.1.call-start = ((), (), s32[]{:S(2)}) async-start(), calls=%async_computation.3 | async-start | bytes 16777216 | tf_op jit(solution)/shard_map/psum | solution.py:62
  329.1 25.7 %all-to-all-start = ((bf16[32,32,256]{2,1,0:T(8,128)(2,1)}), bf16[32,32,256]{2,1,0:T(8,128)(2,1)S(1)}, u32[]{:S(2)}, u32[]{:S(2)}) async-start(bf16[32,32,256]{2,1,0:T(8,128)(2,1)} %bitcast.13), calls=%async_computation.1 | async-start | bytes 1048576 | tf_op jit(solution)/shard_map/all_to_all | solution.py:41
  513.7 7.3 copy-start.66
  513.7 7.3 copy-start.67
  514.4 6.7 copy-start.68
  529.4 1.0 copy-start.28
  583.1 1.0 copy-start.26
  636.0 1.0 copy-start.29
  685.0 1.0 copy-start.27
  733.3 44.4 %copy-start.30 = (f32[4,128,128]{2,1,0:T(8,128)}, f32[4,128,128]{2,1,0:T(8,128)S(1)}, u32[]{:S(2)}) copy-start(f32[4,128,128]{2,1,0:T(8,128)S(1)} %custom-call.58) | copy-start | bytes 786436
  868.7 98.1 %copy-start.25 = (f32[4,256,256]{2,1,0:T(8,128)}, f32[4,256,256]{2,1,0:T(8,128)S(1)}, u32[]{:S(2)}) copy-start(f32[4,256,256]{2,1,0:T(8,128)S(1)} %get-tuple-element.372) | copy-start | bytes 3145732
  1112.6 3.6 copy-start.71
  1220.5 2.7 copy-start.24
  1231.0 0.7 copy-start.47
  1252.8 0.8 copy-start
  1285.5 0.8 copy-start.2
  1318.3 0.8 copy-start.4
  1348.5 3.5 copy-start.23
  1349.2 0.8 copy-start.6
  1381.5 0.8 copy-start.8
  1392.0 0.7 copy-start.52
  1414.2 0.8 copy-start.10
  1446.9 0.8 copy-start.12
  1456.0 0.7 copy-start.54
  1477.1 3.5 copy-start.22
  1477.8 0.8 copy-start.14
  1510.6 0.8 copy-start.16
  1543.2 0.8 copy-start.18
  1575.5 0.8 copy-start.20
  1605.9 2.0 copy-start.31
  1605.9 2.0 copy-start.32
  1606.0 2.0 copy-start.33
  1606.0 3.9 copy-start.1
  1606.0 3.9 copy-start.3
  1606.0 3.9 copy-start.5
  1606.0 3.9 copy-start.7
  1606.0 3.9 copy-start.34
  1606.0 3.9 copy-start.35
  1606.0 3.9 copy-start.36
  1606.0 3.9 copy-start.37
  1606.0 3.9 copy-start.62
  1606.0 3.9 copy-start.63
  1606.1 3.9 copy-start.64
  1606.1 3.9 copy-start.65
  1608.0 2.6 copy-start.9
  1608.0 2.6 copy-start.11
  1608.0 2.6 copy-start.13
  1608.0 2.6 copy-start.15
  1608.0 2.6 copy-start.38
  1608.0 2.6 copy-start.39
  1608.0 2.6 copy-start.40
  1608.0 2.6 copy-start.41
  1608.1 2.6 copy-start.58
  1608.1 2.6 copy-start.59
  1608.1 2.6 copy-start.60
  1608.1 2.6 copy-start.61
  1610.0 1.2 copy-start.17
  1610.0 1.3 copy-start.19
  1610.0 1.4 copy-start.21
  1610.0 1.6 copy-start.42
  1610.0 1.7 copy-start.43
  1610.0 1.9 copy-start.44
  (11 other events, 7.1 us)
Sparse Core Ops, SparseCore 0:
  145.7 148.2 reduce-scatter.1
  302.2 188.3 all-reduce.3
where the time goes:
time: 1630 us; the launch traced here: 1620 us
  other arithmetic  944 us (58%)
  local copies, waits for them, and re-layouts  286 us (18%)
  waiting for transfers between devices  162 us (10%)
  matrix products  131 us (8%)
  blocking collectives  78.7 us (5%)
    another operation x28, other arithmetic, shards(): factor = jnp.linalg.cholesky(mean)  551 us
    another operation x22, other arithmetic, shards(): jax.scipy.linalg.solve_triangular(factor[which], values, lower=True)  329 us
    psum x1, waiting for transfers between devices, shards(): leaf_grams = lax.psum(spread, ('row', 'col'))  132 us
    scatter x1, local copies, waits for them, and re-layouts, shards(): inverse = jnp.zeros((total_rows,), jnp.int32).at[tree_perm].set(jnp.arang...  120 us
    another operation x113, local copies, waits for them, and re-layouts, shards(): jax.scipy.linalg.solve_triangular(factor[which], values, lower=True)  95 us
    psum x1, blocking collectives, shards(): sample_w = lax.psum(partial_w, 'row').astype(jnp.bfloat16)  78.7 us
    another operation x48, matrix products, shards(): jax.scipy.linalg.solve_triangular(factor[which], values, lower=True)  49.2 us
  transfers between devices with their start and end apart: 3, of which 3 were waited for; matrix products, arithmetic and copies ran while one was open for 11% of the time, Pallas kernels for 0%

commit v1 on v0

--- a/solution.py
+++ b/solution.py
@@ -2,6 +2,7 @@
 import jax.numpy as jnp
 from jax import lax
 from jax.sharding import PartitionSpec as P
+from jax.lax import psum
 
 UNIT = 128
 MINU = 4
@@ -59,7 +60,13 @@
     chosen = stored_leaf[None, :] == leaf_range[:, None]
     masked = jnp.where(chosen[:, :, None], sample[None, :, :], jnp.zeros((), jnp.bfloat16))
     spread = jnp.einsum("lrs,rt->lst", masked, sample, preferred_element_type=jnp.float32)
-    leaf_grams = lax.psum(spread, ("row", "col"))
+
+    def list_the_squares(vals):
+        for d in ("col", "row"):
+            vals = psum(vals, d)
+        return vals
+
+    leaf_grams = list_the_squares(spread)
     for level in range(levels):
         group = 2**level
         count = leaves // group

time: 1630 us -> 1870 us (1.15)
  waiting for transfers between devices: 162 us -> 402 us
    psum x1 -> x2, waiting for transfers between devices: 132 us -> 370 us  [list_the_squares(): vals = psum(vals, d)]
  transfers between devices with their start and end apart: 3 -> 4, of which waited for: 3 -> 4; matrix products, arithmetic and copies ran while one was open for 11% -> 9% of each run, Pallas kernels for 0% -> 0%
where the time goes in v1:
time: 1870 us; the launch traced here: 1860 us
  other arithmetic  945 us (51%)
  waiting for transfers between devices  402 us (21%)
  local copies, waits for them, and re-layouts  286 us (15%)
  matrix products  131 us (7%)
  blocking collectives  78.7 us (4%)
    another operation x28, other arithmetic, shards(): factor = jnp.linalg.cholesky(mean)  551 us
    psum x2, waiting for transfers between devices, list_the_squares(): vals = psum(vals, d)  370 us
    another operation x22, other arithmetic, shards(): jax.scipy.linalg.solve_triangular(factor[which], values, lower=True)  329 us
    scatter x1, local copies, waits for them, and re-layouts, shards(): inverse = jnp.zeros((total_rows,), jnp.int32).at[tree_perm].set(jnp.arang...  120 us
    another operation x113, local copies, waits for them, and re-layouts, shards(): jax.scipy.linalg.solve_triangular(factor[which], values, lower=True)  95 us
    psum x1, blocking collectives, shards(): sample_w = lax.psum(partial_w, 'row').astype(jnp.bfloat16)  78.7 us
    another operation x48, matrix products, shards(): jax.scipy.linalg.solve_triangular(factor[which], values, lower=True)  49.2 us
  transfers between devices with their start and end apart: 4, of which 4 were waited for; matrix products, arithmetic and copies ran while one was open for 9% of the time, Pallas kernels for 0%

profile of v1, /device:TPU:0, one launch (start us, length us, event | category | flops | bytes accessed | tf_op | source)
XLA Modules:
  0.0 1862.8 jit_solution(17802566809061573151)
XLA Ops:
  6.5 30.1 %fusion.169 = f32[4096,256]{1,0:T(8,128)} fusion(bf16[8192,4096]{1,0:T(8,128)(2,1)} %param.7, bf16[8192,256]{1,0:T(8,128)(2,1)} %param.8), kind=kOutput, calls=%fused_computation.425 | convolution fusion | flops 17179869184 | bytes 75497472 | tf_op jit(solution)/shard_map/dot_general | solution.py:14
  36.6 78.7 %all-reduce.8 = bf16[4096,256]{1,0:T(8,128)(2,1)S(1)} all-reduce(f32[4096,256]{1,0:T(8,128)} %fusion.169), channel_id=1, replica_groups=mesh['row'=4,'col'=8] {'row'}, use_global_device_ids=true, to_apply=%region_4.5 | all-reduce | flops 1048576 | bytes 6291456 | tf_op jit(solution)/shard_map/psum | solution.py:17
  115.4 30.2 %convolution_bitcast_fusion = f32[8192,256]{0,1:T(8,128)} fusion(bf16[8192,4096]{1,0:T(8,128)(2,1)} %param.7, bf16[4096,256]{1,0:T(8,128)(2,1)S(1)} %all-reduce.8), kind=kOutput, calls=%fused_computation.46 | convolution fusion | flops 17179869184 | bytes 77594624 | tf_op jit(solution)/shard_map/dot_general | solution.py:21
  146.5 120.1 %scatter_custom_fusion = s32[32768]{0:T(1024)S(1)} fusion(s32[32768]{0:T(1024)S(1)} %compare_select_fusion, s32[32768]{0:T(1024)S(1)} %iota.124, s32[]{:T(128)} %copy.191), kind=kCustom, calls=%fused_computation.279 | custom fusion | bytes 131076 | tf_op jit(solution)/shard_map/scatter | solution.py:34
  266.8 27.2 %reduce-scatter.2.cloned.1.call-done = f32[1024,256]{0,1:T(8,128)} async-done(((f32[8192,256]{0,1:T(8,128)}), f32[1024,256]{0,1:T(8,128)}) %reduce-scatter.2.cloned.1.call-update) | async-done | bytes 1048592 | tf_op jit(solution)/shard_map/reduce_scatter | solution.py:20
  295.3 6.8 fusion
  312.3 259.1 %all-reduce.5.cloned.1.call-done = f32[32,256,256]{2,1,0:T(8,128)} async-done(((f32[32,256,256]{2,1,0:T(8,128)}), f32[32,256,256]{2,1,0:T(8,128)}) %all-reduce.5.cloned.1.call-update) | async-done | bytes 8388624 | tf_op jit(solution)/shard_map/psum | solution.py:66
  578.3 3.2 broadcast_compare_fusion.18
  590.7 5.7 scatter_custom_fusion.1
  596.4 3.9 all-to-all-start
  606.0 5.6 broadcast_compare_fusion.3
  611.6 4.9 all-to-all-done
  616.5 3.9 gather_fusion.2
  620.8 110.7 %all-reduce.7.cloned.1.call-done = f32[32,256,256]{2,1,0:T(8,128)} async-done(((f32[32,256,256]{2,1,0:T(8,128)}), f32[32,256,256]{2,1,0:T(8,128)}) %all-reduce.7.cloned.1.call-update) | async-done | bytes 8388624 | tf_op jit(solution)/shard_map/psum | solution.py:66
  731.4 4.2 bitcast_reduce_fusion.1
  739.8 6.5 bitcast_reduce_fusion.2
  750.4 4.1 bitcast_reduce_fusion
  756.4 4.0 gather_fusion
  761.8 4.2 divide_select_fusion.1
  771.9 47.7 %custom-call.37 = f32[4,128,128]{2,1,0:T(8,128)S(1)} custom-call(f32[4,128,128]{2,1,0:T(8,128)} %cholesky.350), custom_call_target="Cholesky" | custom-call | tf_op jit(solution)/shard_map/jit(cholesky)/cholesky | solution.py:90
  825.6 48.5 %custom-call.51 = f32[4,128,128]{2,1,0:T(8,128)} custom-call(f32[4,128,128]{2,1,0:T(8,128)} %cholesky.356), custom_call_target="Cholesky" | custom-call | tf_op jit(solution)/shard_map/jit(cholesky)/cholesky | solution.py:90
  877.8 47.5 %custom-call.44 = f32[4,128,128]{2,1,0:T(8,128)} custom-call(f32[4,128,128]{2,1,0:T(8,128)S(1)} %cholesky.353), custom_call_target="Cholesky" | custom-call | tf_op jit(solution)/shard_map/jit(cholesky)/cholesky | solution.py:90
  926.8 47.3 %custom-call.58 = f32[4,128,128]{2,1,0:T(8,128)S(1)} custom-call(f32[4,128,128]{2,1,0:T(8,128)S(1)} %cholesky.359), custom_call_target="Cholesky" | custom-call | tf_op jit(solution)/shard_map/jit(cholesky)/cholesky | solution.py:90
  976.2 39.3 %custom-call.38 = f32[4,1,128,128]{2,3,1,0:T(8,128)S(1)} custom-call(f32[4,1,128,128]{3,2,1,0:T(8,128)S(1)} %get-tuple-element.324), custom_call_target="InvertDiagBlocksLowerTriangular" | custom-call | tf_op jit(solution)/shard_map/jit(cholesky)/cholesky | solution.py:90
  1018.5 47.5 %custom-call.39 = f32[4,128,128]{2,1,0:T(8,128)} custom-call(f32[4,128,128]{2,1,0:T(8,128)S(1)} %convolution_subtract_fusion.19), custom_call_target="Cholesky" | custom-call | tf_op jit(solution)/shard_map/jit(cholesky)/cholesky | solution.py:90
  1067.1 40.9 %custom-call.45 = f32[4,1,128,128]{2,3,1,0:T(8,128)} custom-call(f32[4,1,128,128]{3,2,1,0:T(8,128)} %get-tuple-element.322), custom_call_target="InvertDiagBlocksLowerTriangular" | custom-call | tf_op jit(solution)/shard_map/jit(cholesky)/cholesky | solution.py:90
  1112.0 48.3 %custom-call.46 = f32[4,128,128]{2,1,0:T(8,128)} custom-call(f32[4,128,128]{2,1,0:T(8,128)} %convolution_subtract_fusion.18), custom_call_target="Cholesky" | custom-call | tf_op jit(solution)/shard_map/jit(cholesky)/cholesky | solution.py:90
  1162.4 40.7 %custom-call.52 = f32[4,1,128,128]{2,3,1,0:T(8,128)} custom-call(f32[4,1,128,128]{3,2,1,0:T(8,128)} %get-tuple-element.321), custom_call_target="InvertDiagBlocksLowerTriangular" | custom-call | tf_op jit(solution)/shard_map/jit(cholesky)/cholesky | solution.py:90
  1207.6 48.5 %custom-call.53 = f32[4,128,128]{2,1,0:T(8,128)} custom-call(f32[4,128,128]{2,1,0:T(8,128)} %convolution_subtract_fusion.17), custom_call_target="Cholesky" | custom-call | tf_op jit(solution)/shard_map/jit(cholesky)/cholesky | solution.py:90
  1257.2 40.8 %custom-call.59 = f32[4,1,128,128]{2,3,1,0:T(8,128)} custom-call(f32[4,1,128,128]{3,2,1,0:T(8,128)} %get-tuple-element.323), custom_call_target="InvertDiagBlocksLowerTriangular" | custom-call | tf_op jit(solution)/shard_map/jit(cholesky)/cholesky | solution.py:90
  1301.7 48.3 %custom-call.60 = f32[4,128,128]{2,1,0:T(8,128)} custom-call(f32[4,128,128]{2,1,0:T(8,128)} %convolution_subtract_fusion.16), custom_call_target="Cholesky" | custom-call | tf_op jit(solution)/shard_map/jit(cholesky)/cholesky | solution.py:90
  1353.4 3.5 select_select_fusion.3
  1357.1 3.8 while.47
  1360.9 20.1 %custom-call.64 = f32[2,128,128]{1,2,0:T(8,128)S(1)} custom-call(f32[2,128,128]{2,1,0:T(8,128)S(1)} %get-tuple-element.120), custom_call_target="InvertDiagBlocksLowerTriangular" | custom-call | tf_op jit(solution)/shard_map/jit(_solve_triangular)/triangular_solve | solution.py:93
  1383.6 4.3 while.46
  1388.0 19.7 %custom-call.63 = f32[2,128,128]{1,2,0:T(8,128)S(1)} custom-call(f32[2,128,128]{2,1,0:T(8,128)S(1)} %get-tuple-element.119), custom_call_target="InvertDiagBlocksLowerTriangular" | custom-call | tf_op jit(solution)/shard_map/jit(_solve_triangular)/triangular_solve | solution.py:93
  1410.3 4.0 while.45
  1414.3 19.7 %custom-call.62 = f32[2,128,128]{1,2,0:T(8,128)S(1)} custom-call(f32[2,128,128]{2,1,0:T(8,128)S(1)} %get-tuple-element.118), custom_call_target="InvertDiagBlocksLowerTriangular" | custom-call | tf_op jit(solution)/shard_map/jit(_solve_triangular)/triangular_solve | solution.py:93
  1436.7 4.2 while.44
  1441.4 19.8 %custom-call.61 = f32[2,128,128]{1,2,0:T(8,128)S(1)} custom-call(f32[2,128,128]{2,1,0:T(8,128)S(1)} %get-tuple-element.117), custom_call_target="InvertDiagBlocksLowerTriangular" | custom-call | tf_op jit(solution)/shard_map/jit(_solve_triangular)/triangular_solve | solution.py:93
  1464.9 6.9 while.43
  1472.5 20.5 %custom-call.57 = f32[2,128,128]{1,2,0:T(8,128)S(1)} custom-call(f32[2,128,128]{2,1,0:T(8,128)} %copy-done.47), custom_call_target="InvertDiagBlocksLowerTriangular" | custom-call | tf_op jit(solution)/shard_map/jit(_solve_triangular)/triangular_solve | solution.py:93
  1497.3 7.2 while.42
  1505.1 20.5 %custom-call.56 = f32[2,128,128]{1,2,0:T(8,128)S(1)} custom-call(f32[2,128,128]{2,1,0:T(8,128)} %copy-done.48), custom_call_target="InvertDiagBlocksLowerTriangular" | custom-call | tf_op jit(solution)/shard_map/jit(_solve_triangular)/triangular_solve | solution.py:93
  1530.0 7.1 while.41
  1537.8 20.7 %custom-call.55 = f32[2,128,128]{1,2,0:T(8,128)S(1)} custom-call(f32[2,128,128]{2,1,0:T(8,128)} %copy-done.49), custom_call_target="InvertDiagBlocksLowerTriangular" | custom-call | tf_op jit(solution)/shard_map/jit(_solve_triangular)/triangular_solve | solution.py:93
  1562.8 5.4 while.40
  1568.8 20.5 %custom-call.54 = f32[2,128,128]{1,2,0:T(8,128)S(1)} custom-call(f32[2,128,128]{2,1,0:T(8,128)} %copy-done.50), custom_call_target="InvertDiagBlocksLowerTriangular" | custom-call | tf_op jit(solution)/shard_map/jit(_solve_triangular)/triangular_solve | solution.py:93
  1593.7 6.8 while.39
  1601.2 20.5 %custom-call.50 = f32[2,128,128]{1,2,0:T(8,128)S(1)} custom-call(f32[2,128,128]{2,1,0:T(8,128)} %copy-done.51), custom_call_target="InvertDiagBlocksLowerTriangular" | custom-call | tf_op jit(solution)/shard_map/jit(_solve_triangular)/triangular_solve | solution.py:93
  1626.0 6.8 while.38
  1633.5 20.9 %custom-call.49 = f32[2,128,128]{1,2,0:T(8,128)S(1)} custom-call(f32[2,128,128]{2,1,0:T(8,128)} %copy-done.52), custom_call_target="InvertDiagBlocksLowerTriangular" | custom-call | tf_op jit(solution)/shard_map/jit(_solve_triangular)/triangular_solve | solution.py:93
  1658.7 7.1 while.37
  1666.5 20.5 %custom-call.48 = f32[2,128,128]{1,2,0:T(8,128)S(1)} custom-call(f32[2,128,128]{2,1,0:T(8,128)} %copy-done.53), custom_call_target="InvertDiagBlocksLowerTriangular" | custom-call | tf_op jit(solution)/shard_map/jit(_solve_triangular)/triangular_solve | solution.py:93
  1691.4 5.4 while.36
  1697.4 20.5 %custom-call.47 = f32[2,128,128]{1,2,0:T(8,128)S(1)} custom-call(f32[2,128,128]{2,1,0:T(8,128)} %copy-done.54), custom_call_target="InvertDiagBlocksLowerTriangular" | custom-call | tf_op jit(solution)/shard_map/jit(_solve_triangular)/triangular_solve | solution.py:93
  1722.3 7.1 while.35
  1730.1 20.6 %custom-call.43 = f32[2,128,128]{1,2,0:T(8,128)S(1)} custom-call(f32[2,128,128]{2,1,0:T(8,128)} %copy-done.55), custom_call_target="InvertDiagBlocksLowerTriangular" | custom-call | tf_op jit(solution)/shard_map/jit(_solve_triangular)/triangular_solve | solution.py:93
  1755.1 7.2 while.34
  1762.9 20.5 %custom-call.42 = f32[2,128,128]{1,2,0:T(8,128)S(1)} custom-call(f32[2,128,128]{2,1,0:T(8,128)} %copy-done.56), custom_call_target="InvertDiagBlocksLowerTriangular" | custom-call | tf_op jit(solution)/shard_map/jit(_solve_triangular)/triangular_solve | solution.py:93
  1787.7 6.8 while.33
  1795.1 20.5 %custom-call.41 = f32[2,128,128]{1,2,0:T(8,128)S(1)} custom-call(f32[2,128,128]{2,1,0:T(8,128)} %copy-done.57), custom_call_target="InvertDiagBlocksLowerTriangular" | custom-call | tf_op jit(solution)/shard_map/jit(_solve_triangular)/triangular_solve | solution.py:93
  1820.0 5.4 while.32
  1826.0 20.7 %custom-call.40 = f32[2,128,128]{1,2,0:T(8,128)S(1)} custom-call(f32[2,128,128]{2,1,0:T(8,128)} %copy-done.46), custom_call_target="InvertDiagBlocksLowerTriangular" | custom-call | tf_op jit(solution)/shard_map/jit(_solve_triangular)/triangular_solve | solution.py:93
  (429 shorter events, 258.9 us)
Async XLA Ops:
  6.5 287.5 %reduce-scatter.2.cloned.1.call-start = ((), (), s32[]{:S(2)}) async-start(), calls=%async_computation.2 | async-start | bytes 9437184 | tf_op jit(solution)/shard_map/reduce_scatter | solution.py:20
  145.6 0.9 copy-start.45
  145.6 425.7 %all-reduce.5.cloned.1.call-start = ((), (), s32[]{:S(2)}) async-start(), calls=%async_computation.3 | async-start | bytes 16777216 | tf_op jit(solution)/shard_map/psum | solution.py:66
  302.1 429.3 %all-reduce.7.cloned.1.call-start = ((), (), s32[]{:S(2)}) async-start(), calls=%async_computation.4 | async-start | bytes 16777216 | tf_op jit(solution)/shard_map/psum | solution.py:66
  596.4 20.1 %all-to-all-start = ((bf16[32,32,256]{2,1,0:T(8,128)(2,1)}), bf16[32,32,256]{2,1,0:T(8,128)(2,1)S(1)}, u32[]{:S(2)}, u32[]{:S(2)}) async-start(bf16[32,32,256]{2,1,0:T(8,128)(2,1)} %bitcast.13), calls=%async_computation.1 | async-start | bytes 1048576 | tf_op jit(solution)/shard_map/all_to_all | solution.py:42
  754.5 7.3 copy-start.66
  754.5 7.3 copy-start.67
  755.1 6.7 copy-start.68
  770.2 1.0 copy-start.28
  823.9 1.0 copy-start.26
  876.8 1.0 copy-start.29
  925.8 1.0 copy-start.27
  974.1 44.4 %copy-start.30 = (f32[4,128,128]{2,1,0:T(8,128)}, f32[4,128,128]{2,1,0:T(8,128)S(1)}, u32[]{:S(2)}) copy-start(f32[4,128,128]{2,1,0:T(8,128)S(1)} %custom-call.58) | copy-start | bytes 786436
  1109.4 98.1 %copy-start.25 = (f32[4,256,256]{2,1,0:T(8,128)}, f32[4,256,256]{2,1,0:T(8,128)S(1)}, u32[]{:S(2)}) copy-start(f32[4,256,256]{2,1,0:T(8,128)S(1)} %get-tuple-element.372) | copy-start | bytes 3145732
  1353.4 3.6 copy-start.71
  1461.3 2.7 copy-start.24
  1471.8 0.7 copy-start.47
  1493.6 0.8 copy-start
  1526.3 0.8 copy-start.2
  1559.1 0.8 copy-start.4
  1589.3 3.5 copy-start.23
  1590.0 0.8 copy-start.6
  1622.3 0.8 copy-start.8
  1632.8 0.7 copy-start.52
  1655.0 0.8 copy-start.10
  1687.7 0.8 copy-start.12
  1717.9 3.5 copy-start.22
  1718.5 0.8 copy-start.14
  1751.4 0.8 copy-start.16
  1784.0 0.8 copy-start.18
  1816.3 0.8 copy-start.20
  1846.7 2.0 copy-start.31
  1846.7 2.0 copy-start.32
  1846.7 2.0 copy-start.33
  1846.7 3.9 copy-start.1
  1846.7 3.9 copy-start.3
  1846.8 3.9 copy-start.5
  1846.8 3.9 copy-start.7
  1846.8 3.9 copy-start.34
  1846.8 3.9 copy-start.35
  1846.8 3.9 copy-start.36
  1846.8 3.9 copy-start.37
  1846.8 3.9 copy-start.62
  1846.8 3.9 copy-start.63
  1846.8 3.9 copy-start.64
  1846.8 3.9 copy-start.65
  1848.8 2.6 copy-start.9
  1848.8 2.6 copy-start.11
  1848.8 2.6 copy-start.13
  1848.8 2.6 copy-start.15
  1848.8 2.6 copy-start.38
  1848.8 2.6 copy-start.39
  1848.8 2.6 copy-start.40
  1848.8 2.6 copy-start.41
  1848.8 2.6 copy-start.58
  1848.8 2.6 copy-start.59
  1848.8 2.6 copy-start.60
  1848.9 2.6 copy-start.61
  1850.8 1.2 copy-start.17
  1850.8 1.3 copy-start.19
  1850.8 1.4 copy-start.21
  1850.8 1.6 copy-start.42
  1850.8 1.7 copy-start.43
  1850.8 1.9 copy-start.44
  (12 other events, 7.7 us)
Sparse Core Ops, SparseCore 0:
  145.7 148.2 reduce-scatter.1
  302.2 269.0 all-reduce.4
  573.8 157.5 all-reduce.6
